TPU v7x, 256 devices: a whole 4x4x8 slice. The times are simulated.
256 devices in a mesh: ang: 64 (over x, z, core), sy: 2 (over y_hi), sx: 2 (over y_lo).
Axes of the slice: x: 4, y: 4 (y_hi: 2, y_lo: 2; y = y_hi * 2 + y_lo), z: 8, core: 2. Of those that a mesh axis runs over, the one named last changes fastest.
Arguments:
- objects: bfloat16 [64, 2, 1024, 1024], P('ang', None, 'sy', 'sx'), may hold values from -4 to 4
- probe: float32 [2, 2, 256, 256], replicated, may hold values from -4 to 4
- data: bfloat16 [64, 2, 2, 2, 256, 256], P('ang', 'sy', 'sx'), may hold values from 0 to 4
- positions: int32 [64, 2, 2, 2, 2], P('ang', 'sy', 'sx'), may hold values from 0 to 384
- block_index: int32 [8, 16], replicated, may hold values from 0 to 511, as said below
- block_values: bfloat16 [8, 16, 128, 128], replicated, may hold values from -0.125 to 0.125
Outputs:
- object_grad: float32 [64, 2, 1024, 1024], P('ang', None, 'sy', 'sx')
- probe_grad: float32 [64, 2, 2, 256, 256], P('ang')
- vol_grad: float32 [2, 512, 2, 1024], P('sy', ('ang', 'sx'))
Inputs may be any that keep to these rules, and one draw needn't show every extreme that they name: `positions`: A position counts cells from 64 cells before the tile's first row or column. `block_index`: entry g names the angle g // 8 and the column block g % 8; every angle is named by exactly 2 entries.
All inputs are finite; a program needn't handle non-finite values.
Results may differ from a plain program's by a relative error of at most 0.011.
Values may be sent and summed in bfloat16 or wider, within the bound.
A program may use at most 64 MiB of HBM per device.

v0:
```python
from functools import partial
import math
import jax
import jax.numpy as jnp
from jax import lax
from jax.sharding import PartitionSpec as P

PATCH = 256
RIM = 64
BLK = 128


def with_halo(cells, sides, width):
    for axis, dim in sides:
        count = lax.axis_size(axis)
        ends = count - 1
        head = lax.slice_in_dim(cells, 0, width, axis=dim)
        tail = lax.slice_in_dim(cells, cells.shape[dim] - width, cells.shape[dim], axis=dim)
        cells = jnp.concatenate(
            [
                lax.ppermute(tail, axis, [(i, (i + 1) % count) for i in range(ends)]),
                cells,
                lax.ppermute(head, axis, [((i + 1) % count, i) for i in range(ends)]),
            ],
            axis=dim,
        )
    return cells


def dft_parts(length):
    sample_ids = jnp.arange(length, dtype=jnp.int32)
    product = sample_ids[:, None] * sample_ids[None, :] % length
    phases = product.astype(jnp.float32) * (2.0 * math.pi / length)
    factor = 1.0 / math.sqrt(length)
    return (jnp.cos(phases) * factor, -jnp.sin(phases) * factor)


def dft_blocks(length):
    real_part, imag_part = dft_parts(length)
    forward = jnp.stack(
        [jnp.stack([real_part, -imag_part], 1), jnp.stack([imag_part, real_part], 1)], 0
    )
    backward = jnp.stack(
        [jnp.stack([real_part, imag_part], 1), jnp.stack([-imag_part, real_part], 1)], 0
    )
    return (forward.astype(jnp.bfloat16), backward.astype(jnp.bfloat16))


def ramp_table(width):
    column_ids = jnp.arange(width, dtype=jnp.int32)
    offsets = column_ids[None, :] - column_ids[:, None]
    odd_cells = offsets % 2 != 0
    scaled = offsets.astype(jnp.float32) * math.pi
    values = jnp.where(odd_cells, -1.0 / jnp.maximum(scaled * scaled, 1.0), 0.0)
    values = jnp.where(offsets == 0, 0.25, values)
    return values.astype(jnp.bfloat16)


def left_product(matrix, fields):
    return jnp.einsum("srtk,btkc->bsrc", matrix, fields, preferred_element_type=jnp.float32)


def right_product(fields, matrix):
    return jnp.einsum("btrc,tcsq->bsrq", fields, matrix, preferred_element_type=jnp.float32)


def cut_window(field, corner):
    return lax.dynamic_slice(
        field, (jnp.int32(0), corner[0], corner[1]), (field.shape[0], PATCH, PATCH)
    )


def patch_gradients(patches, measured, probe, forward, backward):
    patch_count = patches.shape[0]
    mode_count = probe.shape[0]
    side = patches.shape[2]
    object_real = patches[:, 0].astype(jnp.float32)[:, None]
    object_imag = patches[:, 1].astype(jnp.float32)[:, None]
    probe_real = probe[None, :, 0]
    probe_imag = probe[None, :, 1]
    exit_real = probe_real * object_real - probe_imag * object_imag
    exit_imag = probe_real * object_imag + probe_imag * object_real
    exit_waves = (
        jnp.stack([exit_real, exit_imag], 2)
        .reshape(patch_count * mode_count, 2, side, side)
        .astype(jnp.bfloat16)
    )
    half_done = left_product(forward, exit_waves).astype(jnp.bfloat16)
    far_field = right_product(half_done, backward).reshape(patch_count, mode_count, 2, side, side)
    intensity = jnp.sum(far_field * far_field, axis=(1, 2))
    misfit = intensity - measured.astype(jnp.float32)
    weighted = (
        (misfit[:, None, None] * far_field)
        .reshape(patch_count * mode_count, 2, side, side)
        .astype(jnp.bfloat16)
    )
    back_half = left_product(backward, weighted).astype(jnp.bfloat16)
    spread = right_product(back_half, forward).reshape(patch_count, mode_count, 2, side, side)
    chi_real = spread[:, :, 0]
    chi_imag = spread[:, :, 1]
    grad_real = jnp.sum(probe_real * chi_real + probe_imag * chi_imag, axis=1)
    grad_imag = jnp.sum(probe_real * chi_imag - probe_imag * chi_real, axis=1)
    patch_grad = jnp.stack([grad_real, grad_imag], 1)
    probe_real_part = jnp.sum(object_real * chi_real + object_imag * chi_imag, axis=0)
    probe_imag_part = jnp.sum(object_real * chi_imag - object_imag * chi_real, axis=0)
    probe_part = jnp.stack([probe_real_part, probe_imag_part], 1)
    return (patch_grad, probe_part)


def fold_rims(field, axis_at, extent):
    inside = lax.slice_in_dim(field, 2 * RIM, 2 * RIM + extent, axis=axis_at)
    leading = lax.slice_in_dim(field, 0, RIM, axis=axis_at)
    trailing = lax.slice_in_dim(field, extent + 3 * RIM, extent + 4 * RIM, axis=axis_at)
    widths_lead = [(0, 0)] * field.ndim
    widths_lead[axis_at] = (0, extent - RIM)
    widths_trail = [(0, 0)] * field.ndim
    widths_trail[axis_at] = (extent - RIM, 0)
    return inside + jnp.pad(leading, widths_lead) + jnp.pad(trailing, widths_trail)


def body(objects, probe, data, positions, block_index, block_values):
    forward, backward = dft_blocks(PATCH)
    tile_rows = objects.shape[2]
    tile_cols = objects.shape[3]
    padded = with_halo(objects[0], (("sy", 1), ("sx", 2)), RIM)
    starts = positions[0, 0, 0]
    patches = jax.vmap(partial(cut_window, padded))(starts)
    patch_grad, probe_part = patch_gradients(patches, data[0, 0, 0], probe, forward, backward)

    def place_patch(grad_piece, corner):
        empty = jnp.zeros(padded.shape, jnp.float32)
        return lax.dynamic_update_slice(empty, grad_piece, (jnp.int32(0), corner[0], corner[1]))

    running_sum = jnp.sum(jax.vmap(place_patch)(patch_grad, starts), axis=0)
    returned = with_halo(running_sum.astype(jnp.bfloat16), (("sy", 1), ("sx", 2)), RIM).astype(
        running_sum.dtype
    )
    object_grad = fold_rims(fold_rims(returned, 1, tile_rows), 2, tile_cols)
    tile_count = lax.axis_size("sy") * lax.axis_size("sx")
    probe_total = lax.psum(probe_part.astype(jnp.bfloat16), ("sy", "sx")).astype(jnp.float32)
    probe_grad = (probe_total / math.sqrt(starts.shape[0] * tile_count))[None]
    line_blocks = block_values.shape[0]
    width_all = line_blocks * block_values.shape[2]
    angle_count = lax.axis_size("ang")
    column_parts = lax.axis_size("sx")
    rows_here = tile_rows // (angle_count * column_parts)
    ramp_matrix = ramp_table(width_all)
    sinogram = object_grad.astype(jnp.bfloat16)[None]
    ramp_split = ramp_matrix.reshape(column_parts, tile_cols, width_all)
    received = lax.all_to_all(sinogram, ("ang", "sx"), split_axis=2, concat_axis=0, tiled=True)
    shaped = received.reshape(angle_count, column_parts, received.shape[1], rows_here, tile_cols)
    result = jnp.einsum("ascrt,stv->acrv", shaped, ramp_split, preferred_element_type=jnp.float32)
    filtered = result.astype(jnp.bfloat16)
    line_data = filtered.reshape(filtered.shape[0], 2, rows_here, line_blocks, BLK)
    angle_of = block_index // line_blocks
    column_of = block_index % line_blocks
    picked = line_data[angle_of, :, :, column_of, :]
    volume = jnp.einsum(
        "bkcru,bkuv->rcbv", picked, block_values, preferred_element_type=jnp.float32
    )
    vol_grad = volume.reshape(1, rows_here, 2, width_all)
    return (object_grad[None], probe_grad, vol_grad)


def solution(mesh):
    placed = (
        P("ang", None, "sy", "sx"),
        P(),
        P("ang", "sy", "sx", None, None, None),
        P("ang", "sy", "sx", None, None),
        P(),
        P(),
    )
    return jax.shard_map(
        body,
        mesh=mesh,
        in_specs=placed,
        out_specs=(
            P("ang", None, "sy", "sx"),
            P("ang", None, None, None, None),
            P("sy", ("ang", "sx"), None, None),
        ),
        check_vma=False,
    )
```

profile of v0, /device:TPU:2, one launch (start us, length us, event | category | flops | bytes accessed | tf_op | source)
XLA Modules:
  0.0 221.8 jit_solution(13552120313437192784)
XLA Ops:
  7.2 1.1 fusion.79
  8.3 5.1 %collective-permute-start = (bf16[2,64,512]{2,1,0:T(8,128)(2,1)S(1)}, bf16[2,64,512]{2,1,0:T(8,128)(2,1)S(1)}, u32[]{:S(2)}, u32[]{:S(2)}) collective-permute-start(bf16[2,64,512]{2,1,0:T(8,128)(2,1)S(1)} %get-tuple-element.75), channel_id=1, source_target_pairs={{0,2},{1,3},{4,6},{5,7},{8,10},{9,11},{12,14},{13,15},{16,18},{17,... | collective-permute-start | bytes 393224 | tf_op jit(solution)/shard_map/ppermute | solution.py:21
  13.4 1.3 collective-permute-start.1
  18.5 1.3 slice_bitcast_fusion.3
  23.0 3.3 %collective-permute-start.2 = (bf16[2,640,64]{2,1,0:T(8,128)(2,1)}, bf16[2,640,64]{2,1,0:T(8,128)(2,1)}, u32[]{:S(2)}, u32[]{:S(2)}) collective-permute-start(bf16[2,640,64]{2,1,0:T(8,128)(2,1)} %get-tuple-element.71), channel_id=1, source_target_pairs={{0,1},{2,3},{4,5},{6,7},{8,9},{10,11},{12,13},{14,15},{16,17},{18,... | collective-permute-start | bytes 491528 | tf_op jit(solution)/shard_map/ppermute | solution.py:21
  26.3 1.5 collective-permute-start.3
  29.0 1.8 copy.54
  30.8 2.0 maximum_bitcast_fusion.3
  32.9 4.5 %collective-permute-done.3 = bf16[2,640,64]{2,1,0:T(8,128)(2,1)} collective-permute-done((bf16[2,640,64]{2,1,0:T(8,128)(2,1)}, bf16[2,640,64]{2,1,0:T(8,128)(2,1)}, u32[]{:S(2)}, u32[]{:S(2)}) %collective-permute-start.3) | collective-permute-done | bytes 163872 | tf_op jit(solution)/shard_map/ppermute | solution.py:23
  37.4 2.2 pad_maximum_fusion
  39.6 5.8 %while.2 = (s32[]{:T(128)}, bf16[2,640,640]{2,1,0:T(8,128)(2,1)S(1)}, s32[2,3]{1,0:T(2,128)S(1)}, bf16[2,2,256,256]{3,2,1,0:T(8,128)(2,1)}, s32[]{:T(128)}) while((s32[]{:T(128)}, bf16[2,640,640]{2,1,0:T(8,128)(2,1)S(1)}, s32[2,3]{1,0:T(2,128)S(1)}, bf16[2,2,256,256]{3,2,1,0:T(8,128)(2,1)}, s32[]{:T(128)}) %tuple.63), condition=%wide.while_cond, body=%wide.while_body.sunk | while | flops 2 | bytes 525929 | solution.py:68
  40.2 2.2 %bitcast_dynamic-update-slice_fusion.2 = bf16[2,2,256,256]{3,2,1,0:T(8,128)(2,1)} fusion(bf16[2,2,256,256]{3,2,1,0:T(8,128)(2,1)} %get-tuple-element.161, s32[]{:T(128)} %get-tuple-element.158, bf16[2,640,640]{2,1,0:T(8,128)(2,1)S(1)} %get-tuple-element.164, s32[]{:T(128)} %bitcast.203, s32[]{:T(128)} %bitcast.204), kind=kLoop, calls=%fused_computation.1.clone.1 | loop fusion | bytes 525824 | tf_op jit(solution)/shard_map/vmap()/gather
  43.1 2.2 %bitcast_dynamic-update-slice_fusion.2 = bf16[2,2,256,256]{3,2,1,0:T(8,128)(2,1)} fusion(bf16[2,2,256,256]{3,2,1,0:T(8,128)(2,1)} %get-tuple-element.161, s32[]{:T(128)} %get-tuple-element.158, bf16[2,640,640]{2,1,0:T(8,128)(2,1)S(1)} %get-tuple-element.164, s32[]{:T(128)} %bitcast.203, s32[]{:T(128)} %bitcast.204), kind=kLoop, calls=%fused_computation.1.clone.1 | loop fusion | bytes 525824 | tf_op jit(solution)/shard_map/vmap()/gather
  45.4 1.2 bitcast_convert_fusion.4
  47.0 1.3 subtract_convert_fusion
  48.3 5.0 %fusion.15 = (f32[4,256,256]{1,2,0:T(8,128)}, f32[2,256,4,256,1]{3,1,4,2,0:T(8,128)}) fusion(bf16[4,1,256,256]{2,3,1,0:T(8,128)(2,1)} %bitcast.227, bf16[4,1,256,256]{2,3,1,0:T(8,128)(2,1)} %bitcast.226, bf16[1,256,2,256]{3,1,2,0:T(8,128)(2,1)S(1)} %copy-done.10, bf16[1,256,2,256]{3,1,2,0:T(8,128)(2,1)S(1)} %copy-done.9, ...), kind=kOutput, calls=%fused_computation.31 | convolution fusion | flops 1078198272 | bytes 5242880 | tf_op jit(solution)/shard_map/btrc,tcsq->bsrq/dot_general | solution.py:64
  53.3 1.4 bitcast_reduce_fusion
  54.7 1.1 mul.359
  55.8 3.4 %fusion.33 = f32[2,256,4,256,1]{3,1,4,2,0:T(8,128)S(1)} fusion(bf16[2,256,2,256,1]{3,1,2,0,4:T(8,128)(2,1)} %get-tuple-element.89, bf16[1,256,2,256]{3,1,2,0:T(8,128)(2,1)S(1)} %get-tuple-element.80, bf16[1,256,2,256]{3,1,2,0:T(8,128)(2,1)} %copy-done.5, f32[2,256,4,256,1]{3,1,4,2,0:T(8,128)} %get-tuple-element.88, f32[4,256,256]{1,2,0:T(8,128)} %bitcast.218), kind=kOutput, calls=%fused_computation.49 | convolution fusion | flops 1076363264 | bytes 6291456 | tf_op jit(solution)/shard_map/btrc,tcsq->bsrq/dot_general | solution.py:64
  59.2 2.7 %add_reduce_fusion = (bf16[2,256,256]{1,2,0:T(8,128)(2,1)S(1)}, bf16[2,256,256]{1,2,0:T(8,128)(2,1)}, f32[2,256,256]{1,2,0:T(8,128)S(1)}, f32[2,256,256]{1,2,0:T(8,128)S(1)}) fusion(f32[2,2,2,256,256]{3,4,1,0,2:T(8,128)S(1)} %bitcast.212, f32[2,256,256]{1,2,0:T(8,128)} %copy-done.4, f32[2,256,256]{1,2,0:T(8,128)} %copy-done.3, ...), kind=kLoop, calls=%fused_computation.64 | loop fusion | flops 3670016 | bytes 5767168 | tf_op jit(solution)/shard_map/reduce_sum | solution.py:104
  62.0 3.1 %broadcast_in_dim.40 = f32[2,2,640,640]{3,2,1,0:T(8,128)} broadcast(f32[]{:T(128)} %constant.70.clone.1), dimensions={} | broadcast | bytes 6553604 | tf_op jit(solution)/shard_map/vmap(vmap())/broadcast_in_dim;vmap()/broadcast_in_dim | solution.py:132
  65.1 33.3 %while.3 = (s32[]{:T(128)}, f32[2,2,640,640]{3,2,1,0:T(8,128)}, s32[2,4]{1,0:T(2,128)S(1)}, f32[2,2,256,256]{2,3,0,1:T(8,128)S(1)}, s32[]{:T(128)}, /*index=5*/s32[4]{0:T(128)S(1)}, s32[]{:T(128)}) while((s32[]{:T(128)}, f32[2,2,640,640]{3,2,1,0:T(8,128)}, s32[2,4]{1,0:T(2,128)S(1)}, f32[2,2,256,256]{2,3,0,1:T(8,128)S(1)}, s32[]{:T(128)}, ...), condition=%wide.while_cond.1, body=%wide.while_body.1.sunk | while | flops 131101 | bytes 4718791 | solution.py:132
  65.8 3.3 %and_reduce_fusion.2 = pred[]{:T(512)} fusion(s32[4]{0:T(128)S(1)} %get-tuple-element.187, s32[1]{0:T(128)} %bitcast.208, s32[1]{0:T(128)} %bitcast.209, s32[1]{0:T(128)} %bitcast.210, s32[1]{0:T(128)} %bitcast.211), kind=kLoop, calls=%fused_computation.4.clone.1 | loop fusion | flops 27 | bytes 33 | tf_op jit(solution)/shard_map/vmap(vmap())/scatter
  69.3 3.9 %dynamic-slice_select_fusion.2 = f32[1,2,256,256]{3,2,1,0:T(8,128)S(1)} fusion(f32[1,2,256,256]{3,2,1,0:T(8,128)S(1)} %copy.105, f32[2,2,640,640]{3,2,1,0:T(8,128)} %get-tuple-element.176, s32[]{:T(128)} %bitcast.205, s32[]{:T(128)} %bitcast.206, s32[]{:T(128)} %bitcast.207, pred[]{:T(512)} %and_reduce_fusion.2), kind=kLoop, calls=%fused_computation.3.clone.1 | loop fusion | flops 131072 | bytes 1572877 | tf_op jit(solution)/shard_map/vmap(vmap())/scatter
  73.3 8.4 %dynamic-update-slice.8 = f32[2,2,640,640]{3,2,1,0:T(8,128)} dynamic-update-slice(f32[2,2,640,640]{3,2,1,0:T(8,128)} %get-tuple-element.176, f32[1,2,256,256]{3,2,1,0:T(8,128)S(1)} %dynamic-slice_select_fusion.2, s32[]{:T(128)} %bitcast.205, s32[]{:T(128)} %constant.71.clone.1..sunk, s32[]{:T(128)} %bitcast.206, s32[]{:T(128)} %bitcast.207) | dynamic-update-slice | bytes 1048580 | tf_op jit(solution)/shard_map/vmap(vmap())/scatter
  82.4 3.3 %and_reduce_fusion.2 = pred[]{:T(512)} fusion(s32[4]{0:T(128)S(1)} %get-tuple-element.187, s32[1]{0:T(128)} %bitcast.208, s32[1]{0:T(128)} %bitcast.209, s32[1]{0:T(128)} %bitcast.210, s32[1]{0:T(128)} %bitcast.211), kind=kLoop, calls=%fused_computation.4.clone.1 | loop fusion | flops 27 | bytes 33 | tf_op jit(solution)/shard_map/vmap(vmap())/scatter
  85.9 3.9 %dynamic-slice_select_fusion.2 = f32[1,2,256,256]{3,2,1,0:T(8,128)S(1)} fusion(f32[1,2,256,256]{3,2,1,0:T(8,128)S(1)} %copy.105, f32[2,2,640,640]{3,2,1,0:T(8,128)} %get-tuple-element.176, s32[]{:T(128)} %bitcast.205, s32[]{:T(128)} %bitcast.206, s32[]{:T(128)} %bitcast.207, pred[]{:T(512)} %and_reduce_fusion.2), kind=kLoop, calls=%fused_computation.3.clone.1 | loop fusion | flops 131072 | bytes 1572877 | tf_op jit(solution)/shard_map/vmap(vmap())/scatter
  89.8 8.6 %dynamic-update-slice.8 = f32[2,2,640,640]{3,2,1,0:T(8,128)} dynamic-update-slice(f32[2,2,640,640]{3,2,1,0:T(8,128)} %get-tuple-element.176, f32[1,2,256,256]{3,2,1,0:T(8,128)S(1)} %dynamic-slice_select_fusion.2, s32[]{:T(128)} %bitcast.205, s32[]{:T(128)} %constant.71.clone.1..sunk, s32[]{:T(128)} %bitcast.206, s32[]{:T(128)} %bitcast.207) | dynamic-update-slice | bytes 1048580 | tf_op jit(solution)/shard_map/vmap(vmap())/scatter
  98.4 3.8 %reduce_sum.66 = bf16[2,640,640]{2,1,0:T(8,128)(2,1)S(1)} reduce(f32[2,2,640,640]{3,2,1,0:T(8,128)} %get-tuple-element.16, f32[]{:T(128)} %constant.70.clone.1), dimensions={0}, to_apply=%region_5.6 | reduce | flops 819200 | bytes 8192004 | tf_op jit(solution)/shard_map/reduce_sum | solution.py:134
  102.2 5.6 %collective-permute-start.4 = (bf16[2,64,640]{2,1,0:T(8,128)(2,1)S(1)}, bf16[2,64,640]{2,1,0:T(8,128)(2,1)S(1)}, u32[]{:S(2)}, u32[]{:S(2)}) collective-permute-start(bf16[2,64,640]{2,1,0:T(8,128)(2,1)S(1)} %get-tuple-element.69), channel_id=1, source_target_pairs={{0,2},{1,3},{4,6},{5,7},{8,10},{9,11},{12,14},{13,15},{16,18},{17,... | collective-permute-start | bytes 491528 | tf_op jit(solution)/shard_map/ppermute | solution.py:21
  107.9 1.3 collective-permute-start.5
  109.2 1.5 collective-permute-done.4
  110.7 6.3 %collective-permute-done.5 = bf16[2,64,640]{2,1,0:T(8,128)(2,1)S(1)} collective-permute-done((bf16[2,64,640]{2,1,0:T(8,128)(2,1)S(1)}, bf16[2,64,640]{2,1,0:T(8,128)(2,1)S(1)}, u32[]{:S(2)}, u32[]{:S(2)}) %collective-permute-start.5) | collective-permute-done | bytes 163872 | tf_op jit(solution)/shard_map/ppermute | solution.py:23
  117.1 1.3 collective-permute-start.6
  118.5 1.3 collective-permute-start.7
  119.8 4.3 %collective-permute-done.6 = bf16[2,768,64]{2,1,0:T(8,128)(2,1)S(1)} collective-permute-done((bf16[2,768,64]{2,1,0:T(8,128)(2,1)S(1)}, bf16[2,768,64]{2,1,0:T(8,128)(2,1)S(1)}, u32[]{:S(2)}, u32[]{:S(2)}) %collective-permute-start.6) | collective-permute-done | bytes 196640 | tf_op jit(solution)/shard_map/ppermute | solution.py:21
  124.1 4.1 %collective-permute-done.7 = bf16[2,768,64]{2,1,0:T(8,128)(2,1)S(1)} collective-permute-done((bf16[2,768,64]{2,1,0:T(8,128)(2,1)S(1)}, bf16[2,768,64]{2,1,0:T(8,128)(2,1)S(1)}, u32[]{:S(2)}, u32[]{:S(2)}) %collective-permute-start.7) | collective-permute-done | bytes 196640 | tf_op jit(solution)/shard_map/ppermute | solution.py:23
  128.3 2.0 maximum_convert_fusion
  131.0 1.8 convert_bitcast_fusion
  132.7 2.1 copy.59
  134.8 14.4 %all-to-all-start = ((bf16[1,2,512,512]{3,1,0,2:T(2,128)(2,1)}), bf16[1,2,512,512]{3,1,0,2:T(2,128)(2,1)S(1)}, u32[]{:S(2)}, u32[]{:S(2)}) async-start(bf16[1,2,512,512]{3,1,0,2:T(2,128)(2,1)} %copy.59), calls=%async_computation | async-start | bytes 2097152 | tf_op jit(solution)/shard_map/all_to_all | solution.py:150
  150.3 50.9 %all-reduce.4.cloned.1.call-done = bf16[2,2,256,256]{2,3,0,1:T(8,128)(2,1)} async-done(((bf16[2,2,256,256]{2,3,0,1:T(8,128)(2,1)}), bf16[2,2,256,256]{2,3,0,1:T(8,128)(2,1)}) %all-reduce.4.cloned.1.call-update) | async-done | bytes 524304 | tf_op jit(solution)/shard_map/psum | solution.py:140
  201.2 1.1 multiply_bitcast_fusion
  202.3 1.3 copy.66
  204.1 4.6 %bitcast_convert_fusion = bf16[64,2,4,1024]{3,0,2,1:T(8,128)(2,1)S(1)} fusion(s32[2,512]{1,0:T(2,128)S(1)} %multiply_add_fusion, bf16[64,2,2,4,512]{4,3,2,1,0:T(4,128)(2,1)S(1)} %bitcast.222), kind=kOutput, calls=%fused_computation.33 | convolution fusion | flops 1097334784 | bytes 2101248 | tf_op jit(solution)/shard_map/ascrt,stv->acrv/dot_general | solution.py:152
  209.0 1.4 copy.62
  210.3 1.0 gather_fusion
  211.3 2.9 %fusion.30 = f32[4,2,8,128]{3,0,1,2:T(4,128)S(1)} fusion(bf16[8,16,2,4,128]{4,3,2,1,0:T(4,128)(2,1)S(1)} %bitcast.221, bf16[8,16,128,128]{3,2,1,0:T(8,128)(2,1)} %param.11), kind=kOutput, calls=%fused_computation.48 | convolution fusion | flops 33554432 | bytes 4489216 | tf_op jit(solution)/shard_map/bkcru,bkuv->rcbv/dot_general | solution.py:158
  (80 shorter events, 15.2 us)
Async XLA Ops:
  7.2 14.8 %copy-start = (bf16[1,2,512,512]{3,2,1,0:T(8,128)(2,1)S(1)}, bf16[1,2,512,512]{3,2,1,0:T(8,128)(2,1)}, u32[]{:S(2)}) copy-start(bf16[1,2,512,512]{3,2,1,0:T(8,128)(2,1)} %param.6) | copy-start | bytes 3145732
  8.3 13.0 %collective-permute-start = (bf16[2,64,512]{2,1,0:T(8,128)(2,1)S(1)}, bf16[2,64,512]{2,1,0:T(8,128)(2,1)S(1)}, u32[]{:S(2)}, u32[]{:S(2)}) collective-permute-start(bf16[2,64,512]{2,1,0:T(8,128)(2,1)S(1)} %get-tuple-element.75), channel_id=1, source_target_pairs={{0,2},{1,3},{4,6},{5,7},{8,10},{9,11},{12,14},{13,15},{16,18},{17,... | collective-permute-start | bytes 393224 | tf_op jit(solution)/shard_map/ppermute | solution.py:21
  13.4 8.4 %collective-permute-start.1 = (bf16[2,64,512]{2,1,0:T(8,128)(2,1)S(1)}, bf16[2,64,512]{2,1,0:T(8,128)(2,1)S(1)}, u32[]{:S(2)}, u32[]{:S(2)}) collective-permute-start(bf16[2,64,512]{2,1,0:T(8,128)(2,1)S(1)} %get-tuple-element.76), channel_id=1, source_target_pairs={{2,0},{3,1},{6,4},{7,5},{10,8},{11,9},{14,12},{15,13},{18,16},{19,... | collective-permute-start | bytes 393224 | tf_op jit(solution)/shard_map/ppermute | solution.py:23
  21.3 11.6 %copy-start.5 = (bf16[1,256,2,256]{3,1,2,0:T(8,128)(2,1)}, bf16[1,256,2,256]{3,1,2,0:T(8,128)(2,1)S(1)}, u32[]{:S(2)}) copy-start(bf16[1,256,2,256]{3,1,2,0:T(8,128)(2,1)S(1)} %get-tuple-element.83) | copy-start | bytes 786436
  21.3 11.6 %copy-start.8 = (bf16[1,256,2,256]{3,1,2,0:T(8,128)(2,1)}, bf16[1,256,2,256]{3,1,2,0:T(8,128)(2,1)S(1)}, u32[]{:S(2)}) copy-start(bf16[1,256,2,256]{3,1,2,0:T(8,128)(2,1)S(1)} %get-tuple-element.79) | copy-start | bytes 786436
  21.3 0.7 copy-start.11
  22.0 1.0 copy-start.12
  23.0 9.9 %collective-permute-start.2 = (bf16[2,640,64]{2,1,0:T(8,128)(2,1)}, bf16[2,640,64]{2,1,0:T(8,128)(2,1)}, u32[]{:S(2)}, u32[]{:S(2)}) collective-permute-start(bf16[2,640,64]{2,1,0:T(8,128)(2,1)} %get-tuple-element.71), channel_id=1, source_target_pairs={{0,1},{2,3},{4,5},{6,7},{8,9},{10,11},{12,13},{14,15},{16,17},{18,... | collective-permute-start | bytes 491528 | tf_op jit(solution)/shard_map/ppermute | solution.py:21
  26.3 11.1 %collective-permute-start.3 = (bf16[2,640,64]{2,1,0:T(8,128)(2,1)}, bf16[2,640,64]{2,1,0:T(8,128)(2,1)}, u32[]{:S(2)}, u32[]{:S(2)}) collective-permute-start(bf16[2,640,64]{2,1,0:T(8,128)(2,1)} %get-tuple-element.72), channel_id=1, source_target_pairs={{1,0},{3,2},{5,4},{7,6},{9,8},{11,10},{13,12},{15,14},{17,16},{19,... | collective-permute-start | bytes 491528 | tf_op jit(solution)/shard_map/ppermute | solution.py:23
  39.5 7.4 %copy-start.1 = (f32[2,256,256]{1,2,0:T(8,128)S(1)}, f32[2,256,256]{1,2,0:T(8,128)}, u32[]{:S(2)}) copy-start(f32[2,256,256]{1,2,0:T(8,128)} %copy.50) | copy-start | bytes 1572868
  45.4 2.9 %copy-start.9 = (bf16[1,256,2,256]{3,1,2,0:T(8,128)(2,1)S(1)}, bf16[1,256,2,256]{3,1,2,0:T(8,128)(2,1)}, u32[]{:S(2)}) copy-start(bf16[1,256,2,256]{3,1,2,0:T(8,128)(2,1)} %copy-done.8) | copy-start | bytes 786436
  45.4 2.9 %copy-start.10 = (bf16[1,256,2,256]{3,1,2,0:T(8,128)(2,1)S(1)}, bf16[1,256,2,256]{3,1,2,0:T(8,128)(2,1)}, u32[]{:S(2)}) copy-start(bf16[1,256,2,256]{3,1,2,0:T(8,128)(2,1)} %get-tuple-element.84) | copy-start | bytes 786436
  46.8 6.5 %copy-start.3 = (f32[2,256,256]{1,2,0:T(8,128)}, f32[2,256,256]{1,2,0:T(8,128)S(1)}, u32[]{:S(2)}) copy-start(f32[2,256,256]{1,2,0:T(8,128)S(1)} %copy.49) | copy-start | bytes 1572868
  47.0 6.3 %copy-start.4 = (f32[2,256,256]{1,2,0:T(8,128)}, f32[2,256,256]{1,2,0:T(8,128)S(1)}, u32[]{:S(2)}) copy-start(f32[2,256,256]{1,2,0:T(8,128)S(1)} %copy.51) | copy-start | bytes 1572868
  48.3 6.4 %copy-start.6 = (bf16[1,1,1,2,256,256]{4,5,3,2,1,0:T(8,128)(2,1)S(1)}, bf16[1,1,1,2,256,256]{4,5,3,2,1,0:T(8,128)(2,1)}, u32[]{:S(2)}) copy-start(bf16[1,1,1,2,256,256]{4,5,3,2,1,0:T(8,128)(2,1)} %copy.54) | copy-start | bytes 786436
  55.8 3.4 %copy-start.2 = (f32[2,256,256]{1,2,0:T(8,128)S(1)}, f32[2,256,256]{1,2,0:T(8,128)}, u32[]{:S(2)}) copy-start(f32[2,256,256]{1,2,0:T(8,128)} %copy.50) | copy-start | bytes 1572868
  62.0 3.2 %copy-start.13 = (s32[4]{0:T(128)S(1)}, s32[4]{0:T(128)}, u32[]{:S(2)}) copy-start(s32[4]{0:T(128)} %constant.300) | copy-start | bytes 52
  102.2 8.4 %collective-permute-start.4 = (bf16[2,64,640]{2,1,0:T(8,128)(2,1)S(1)}, bf16[2,64,640]{2,1,0:T(8,128)(2,1)S(1)}, u32[]{:S(2)}, u32[]{:S(2)}) collective-permute-start(bf16[2,64,640]{2,1,0:T(8,128)(2,1)S(1)} %get-tuple-element.69), channel_id=1, source_target_pairs={{0,2},{1,3},{4,6},{5,7},{8,10},{9,11},{12,14},{13,15},{16,18},{17,... | collective-permute-start | bytes 491528 | tf_op jit(solution)/shard_map/ppermute | solution.py:21
  107.9 9.1 %collective-permute-start.5 = (bf16[2,64,640]{2,1,0:T(8,128)(2,1)S(1)}, bf16[2,64,640]{2,1,0:T(8,128)(2,1)S(1)}, u32[]{:S(2)}, u32[]{:S(2)}) collective-permute-start(bf16[2,64,640]{2,1,0:T(8,128)(2,1)S(1)} %get-tuple-element.70), channel_id=1, source_target_pairs={{2,0},{3,1},{6,4},{7,5},{10,8},{11,9},{14,12},{15,13},{18,16},{19,... | collective-permute-start | bytes 491528 | tf_op jit(solution)/shard_map/ppermute | solution.py:23
  117.1 6.9 %collective-permute-start.6 = (bf16[2,768,64]{2,1,0:T(8,128)(2,1)S(1)}, bf16[2,768,64]{2,1,0:T(8,128)(2,1)S(1)}, u32[]{:S(2)}, u32[]{:S(2)}) collective-permute-start(bf16[2,768,64]{2,1,0:T(8,128)(2,1)S(1)} %get-tuple-element.67), channel_id=1, source_target_pairs={{0,1},{2,3},{4,5},{6,7},{8,9},{10,11},{12,13},{14,15},{16,17},{18,... | collective-permute-start | bytes 589832 | tf_op jit(solution)/shard_map/ppermute | solution.py:21
  118.5 9.7 %collective-permute-start.7 = (bf16[2,768,64]{2,1,0:T(8,128)(2,1)S(1)}, bf16[2,768,64]{2,1,0:T(8,128)(2,1)S(1)}, u32[]{:S(2)}, u32[]{:S(2)}) collective-permute-start(bf16[2,768,64]{2,1,0:T(8,128)(2,1)S(1)} %get-tuple-element.68), channel_id=1, source_target_pairs={{1,0},{3,2},{5,4},{7,6},{9,8},{11,10},{13,12},{15,14},{17,16},{19,... | collective-permute-start | bytes 589832 | tf_op jit(solution)/shard_map/ppermute | solution.py:23
  128.3 2.0 copy-start.15
  132.7 16.5 %copy-start.7 = (bf16[2,256,256]{1,2,0:T(8,128)(2,1)S(1)}, bf16[2,256,256]{1,2,0:T(8,128)(2,1)}, u32[]{:S(2)}) copy-start(bf16[2,256,256]{1,2,0:T(8,128)(2,1)} %get-tuple-element.34) | copy-start | bytes 786436
  132.7 17.4 %copy-start.14 = (s32[8,16]{1,0:T(8,128)S(1)}, s32[8,16]{1,0:T(8,128)}, u32[]{:S(2)}) copy-start(s32[8,16]{1,0:T(8,128)} %param.10) | copy-start | bytes 1540
  134.8 68.8 %all-to-all-start = ((bf16[1,2,512,512]{3,1,0,2:T(2,128)(2,1)}), bf16[1,2,512,512]{3,1,0,2:T(2,128)(2,1)S(1)}, u32[]{:S(2)}, u32[]{:S(2)}) async-start(bf16[1,2,512,512]{3,1,0,2:T(2,128)(2,1)} %copy.59), calls=%async_computation | async-start | bytes 2097152 | tf_op jit(solution)/shard_map/all_to_all | solution.py:150
  149.2 52.0 %all-reduce.4.cloned.1.call-start = ((), (), s32[]{:S(2)}) async-start(), calls=%async_computation.1 | async-start | bytes 1048576 | tf_op jit(solution)/shard_map/psum | solution.py:140
Sparse Core Ops, SparseCore 0:
  152.9 48.2 all-reduce.3
where the time goes:
time: 223 us; the launch traced here: 222 us
  waiting for transfers between devices  72.1 us (32%)
  local copies, waits for them, and re-layouts  42.3 us (19%)
  other arithmetic  41.9 us (19%)
  starting transfers between devices  35.1 us (16%)
  matrix products  16 us (7%)
  between operations  14.4 us (6%)
    psum x1, waiting for transfers between devices, body(): lax.psum(probe_part.astype(jnp.bfloat16), ('sy', 'sx')).astype(jnp.float32)  50.9 us
    scatter x10, local copies, waits for them, and re-layouts  18.8 us
    ppermute x4, starting transfers between devices, with_halo(): lax.ppermute(tail, axis, [(i, (i + 1) % count) for i in range(ends)])  15.3 us
    ppermute x4, waiting for transfers between devices, with_halo(): lax.ppermute(head, axis, [((i + 1) % count, i) for i in range(ends)])  15.3 us
    scatter x4, other arithmetic  14.4 us
    all_to_all x1, starting transfers between devices, body(): lax.all_to_all(sinogram, ('ang', 'sx'), split_axis=2, concat_axis=0, tile...  14.4 us
    dot_general x2, matrix products, right_product(): jnp.einsum('btrc,tcsq->bsrq', fields, matrix, preferred_element_type=jnp....  8.42 us
    ppermute x4, waiting for transfers between devices, with_halo(): lax.ppermute(tail, axis, [(i, (i + 1) % count) for i in range(ends)])  5.81 us
  transfers between devices with their start and end apart: 10, of which 7 were waited for; matrix products, arithmetic and copies ran while one was open for 7% of the time, Pallas kernels for 0%

commit v1 on v0

--- a/solution.py
+++ b/solution.py
@@ -137,7 +137,9 @@
     )
     object_grad = fold_rims(fold_rims(returned, 1, tile_rows), 2, tile_cols)
     tile_count = lax.axis_size("sy") * lax.axis_size("sx")
-    probe_total = lax.psum(probe_part.astype(jnp.bfloat16), ("sy", "sx")).astype(jnp.float32)
+    probe_total = lax.psum(lax.psum(probe_part.astype(jnp.bfloat16), "sx"), "sy").astype(
+        jnp.float32
+    )
     probe_grad = (probe_total / math.sqrt(starts.shape[0] * tile_count))[None]
     line_blocks = block_values.shape[0]
     width_all = line_blocks * block_values.shape[2]

time: 223 us -> 263 us (1.18)
  waiting for transfers between devices: 72.1 us -> 111 us
    psum x1 -> x2, waiting for transfers between devices: 50.9 us -> 90.1 us  [the longest x1 45.4 us: body(): lax.psum(lax.psum(probe_part.astype(jnp.bfloat16), 'sx'), 'sy')]
  transfers between devices with their start and end apart: 10 -> 11, of which waited for: 7 -> 8; matrix products, arithmetic and copies ran while one was open for 7% -> 6% of each run, Pallas kernels for 0% -> 0%
where the time goes in v1:
time: 263 us; the launch traced here: 261 us
  waiting for transfers between devices  111 us (42%)
  local copies, waits for them, and re-layouts  42.3 us (16%)
  other arithmetic  41.9 us (16%)
  starting transfers between devices  35.2 us (13%)
  matrix products  16 us (6%)
  between operations  14.4 us (5%)
    psum x1, waiting for transfers between devices, body(): lax.psum(lax.psum(probe_part.astype(jnp.bfloat16), 'sx'), 'sy')  45.4 us
    psum x1, waiting for transfers between devices, body(): lax.psum(probe_part.astype(jnp.bfloat16), 'sx')  44.7 us
    scatter x10, local copies, waits for them, and re-layouts  18.8 us
    ppermute x4, starting transfers between devices, with_halo(): lax.ppermute(tail, axis, [(i, (i + 1) % count) for i in range(ends)])  15.3 us
    ppermute x4, waiting for transfers between devices, with_halo(): lax.ppermute(head, axis, [((i + 1) % count, i) for i in range(ends)])  15.3 us
    scatter x4, other arithmetic  14.4 us
    all_to_all x1, starting transfers between devices, body(): lax.all_to_all(sinogram, ('ang', 'sx'), split_axis=2, concat_axis=0, tile...  14.4 us
    dot_general x2, matrix products, right_product(): jnp.einsum('btrc,tcsq->bsrq', fields, matrix, preferred_element_type=jnp....  8.42 us
  transfers between devices with their start and end apart: 11, of which 8 were waited for; matrix products, arithmetic and copies ran while one was open for 6% of the time, Pallas kernels for 0%

profile of v1, /device:TPU:2, one launch (start us, length us, event | category | flops | bytes accessed | tf_op | source)
XLA Modules:
  0.0 261.0 jit_solution(15523240690853105973)
XLA Ops:
  7.2 1.1 fusion.79
  8.3 5.1 %collective-permute-start = (bf16[2,64,512]{2,1,0:T(8,128)(2,1)S(1)}, bf16[2,64,512]{2,1,0:T(8,128)(2,1)S(1)}, u32[]{:S(2)}, u32[]{:S(2)}) collective-permute-start(bf16[2,64,512]{2,1,0:T(8,128)(2,1)S(1)} %get-tuple-element.75), channel_id=1, source_target_pairs={{0,2},{1,3},{4,6},{5,7},{8,10},{9,11},{12,14},{13,15},{16,18},{17,... | collective-permute-start | bytes 393224 | tf_op jit(solution)/shard_map/ppermute | solution.py:21
  13.4 1.3 collective-permute-start.1
  18.5 1.3 slice_bitcast_fusion.3
  23.0 3.3 %collective-permute-start.2 = (bf16[2,640,64]{2,1,0:T(8,128)(2,1)}, bf16[2,640,64]{2,1,0:T(8,128)(2,1)}, u32[]{:S(2)}, u32[]{:S(2)}) collective-permute-start(bf16[2,640,64]{2,1,0:T(8,128)(2,1)} %get-tuple-element.71), channel_id=1, source_target_pairs={{0,1},{2,3},{4,5},{6,7},{8,9},{10,11},{12,13},{14,15},{16,17},{18,... | collective-permute-start | bytes 491528 | tf_op jit(solution)/shard_map/ppermute | solution.py:21
  26.3 1.5 collective-permute-start.3
  29.0 1.8 copy.54
  30.8 2.0 maximum_bitcast_fusion.3
  32.9 4.5 %collective-permute-done.3 = bf16[2,640,64]{2,1,0:T(8,128)(2,1)} collective-permute-done((bf16[2,640,64]{2,1,0:T(8,128)(2,1)}, bf16[2,640,64]{2,1,0:T(8,128)(2,1)}, u32[]{:S(2)}, u32[]{:S(2)}) %collective-permute-start.3) | collective-permute-done | bytes 163872 | tf_op jit(solution)/shard_map/ppermute | solution.py:23
  37.4 2.2 pad_maximum_fusion
  39.6 5.8 %while.2 = (s32[]{:T(128)}, bf16[2,640,640]{2,1,0:T(8,128)(2,1)S(1)}, s32[2,3]{1,0:T(2,128)S(1)}, bf16[2,2,256,256]{3,2,1,0:T(8,128)(2,1)}, s32[]{:T(128)}) while((s32[]{:T(128)}, bf16[2,640,640]{2,1,0:T(8,128)(2,1)S(1)}, s32[2,3]{1,0:T(2,128)S(1)}, bf16[2,2,256,256]{3,2,1,0:T(8,128)(2,1)}, s32[]{:T(128)}) %tuple.63), condition=%wide.while_cond, body=%wide.while_body.sunk | while | flops 2 | bytes 525929 | solution.py:68
  40.2 2.2 bitcast_dynamic-update-slice_fusion.2
  43.1 2.2 bitcast_dynamic-update-slice_fusion.2
  45.4 1.2 bitcast_convert_fusion.4
  47.0 1.3 subtract_convert_fusion
  48.3 5.0 %fusion.15 = (f32[4,256,256]{1,2,0:T(8,128)}, f32[2,256,4,256,1]{3,1,4,2,0:T(8,128)}) fusion(bf16[4,1,256,256]{2,3,1,0:T(8,128)(2,1)} %bitcast.227, bf16[4,1,256,256]{2,3,1,0:T(8,128)(2,1)} %bitcast.226, bf16[1,256,2,256]{3,1,2,0:T(8,128)(2,1)S(1)} %copy-done.10, bf16[1,256,2,256]{3,1,2,0:T(8,128)(2,1)S(1)} %copy-done.9, ...), kind=kOutput, calls=%fused_computation.31 | convolution fusion | flops 1078198272 | bytes 5242880 | tf_op jit(solution)/shard_map/btrc,tcsq->bsrq/dot_general | solution.py:64
  53.3 1.4 bitcast_reduce_fusion
  54.7 1.1 mul.359
  55.8 3.4 %fusion.33 = f32[2,256,4,256,1]{3,1,4,2,0:T(8,128)S(1)} fusion(bf16[2,256,2,256,1]{3,1,2,0,4:T(8,128)(2,1)} %get-tuple-element.89, bf16[1,256,2,256]{3,1,2,0:T(8,128)(2,1)S(1)} %get-tuple-element.80, bf16[1,256,2,256]{3,1,2,0:T(8,128)(2,1)} %copy-done.5, f32[2,256,4,256,1]{3,1,4,2,0:T(8,128)} %get-tuple-element.88, f32[4,256,256]{1,2,0:T(8,128)} %bitcast.218), kind=kOutput, calls=%fused_computation.49 | convolution fusion | flops 1076363264 | bytes 6291456 | tf_op jit(solution)/shard_map/btrc,tcsq->bsrq/dot_general | solution.py:64
  59.2 2.7 %add_reduce_fusion = (bf16[2,256,256]{1,2,0:T(8,128)(2,1)S(1)}, bf16[2,256,256]{1,2,0:T(8,128)(2,1)}, f32[2,256,256]{1,2,0:T(8,128)S(1)}, f32[2,256,256]{1,2,0:T(8,128)S(1)}) fusion(f32[2,2,2,256,256]{3,4,1,0,2:T(8,128)S(1)} %bitcast.212, f32[2,256,256]{1,2,0:T(8,128)} %copy-done.4, f32[2,256,256]{1,2,0:T(8,128)} %copy-done.3, ...), kind=kLoop, calls=%fused_computation.64 | loop fusion | flops 3670016 | bytes 5767168 | tf_op jit(solution)/shard_map/reduce_sum | solution.py:104
  62.0 3.1 %broadcast_in_dim.40 = f32[2,2,640,640]{3,2,1,0:T(8,128)} broadcast(f32[]{:T(128)} %constant.70.clone.1), dimensions={} | broadcast | bytes 6553604 | tf_op jit(solution)/shard_map/vmap(vmap())/broadcast_in_dim;vmap()/broadcast_in_dim | solution.py:132
  65.1 33.3 %while.3 = (s32[]{:T(128)}, f32[2,2,640,640]{3,2,1,0:T(8,128)}, s32[2,4]{1,0:T(2,128)S(1)}, f32[2,2,256,256]{2,3,0,1:T(8,128)S(1)}, s32[]{:T(128)}, /*index=5*/s32[4]{0:T(128)S(1)}, s32[]{:T(128)}) while((s32[]{:T(128)}, f32[2,2,640,640]{3,2,1,0:T(8,128)}, s32[2,4]{1,0:T(2,128)S(1)}, f32[2,2,256,256]{2,3,0,1:T(8,128)S(1)}, s32[]{:T(128)}, ...), condition=%wide.while_cond.1, body=%wide.while_body.1.sunk | while | flops 131101 | bytes 4718791 | solution.py:132
  65.8 3.3 %and_reduce_fusion.2 = pred[]{:T(512)} fusion(s32[4]{0:T(128)S(1)} %get-tuple-element.187, s32[1]{0:T(128)} %bitcast.208, s32[1]{0:T(128)} %bitcast.209, s32[1]{0:T(128)} %bitcast.210, s32[1]{0:T(128)} %bitcast.211), kind=kLoop, calls=%fused_computation.4.clone.1 | loop fusion | flops 27 | bytes 33 | tf_op jit(solution)/shard_map/vmap(vmap())/scatter
  69.3 3.9 %dynamic-slice_select_fusion.2 = f32[1,2,256,256]{3,2,1,0:T(8,128)S(1)} fusion(f32[1,2,256,256]{3,2,1,0:T(8,128)S(1)} %copy.105, f32[2,2,640,640]{3,2,1,0:T(8,128)} %get-tuple-element.176, s32[]{:T(128)} %bitcast.205, s32[]{:T(128)} %bitcast.206, s32[]{:T(128)} %bitcast.207, pred[]{:T(512)} %and_reduce_fusion.2), kind=kLoop, calls=%fused_computation.3.clone.1 | loop fusion | flops 131072 | bytes 1572877 | tf_op jit(solution)/shard_map/vmap(vmap())/scatter
  73.3 8.4 %dynamic-update-slice.8 = f32[2,2,640,640]{3,2,1,0:T(8,128)} dynamic-update-slice(f32[2,2,640,640]{3,2,1,0:T(8,128)} %get-tuple-element.176, f32[1,2,256,256]{3,2,1,0:T(8,128)S(1)} %dynamic-slice_select_fusion.2, s32[]{:T(128)} %bitcast.205, s32[]{:T(128)} %constant.71.clone.1..sunk, s32[]{:T(128)} %bitcast.206, s32[]{:T(128)} %bitcast.207) | dynamic-update-slice | bytes 1048580 | tf_op jit(solution)/shard_map/vmap(vmap())/scatter
  82.4 3.3 %and_reduce_fusion.2 = pred[]{:T(512)} fusion(s32[4]{0:T(128)S(1)} %get-tuple-element.187, s32[1]{0:T(128)} %bitcast.208, s32[1]{0:T(128)} %bitcast.209, s32[1]{0:T(128)} %bitcast.210, s32[1]{0:T(128)} %bitcast.211), kind=kLoop, calls=%fused_computation.4.clone.1 | loop fusion | flops 27 | bytes 33 | tf_op jit(solution)/shard_map/vmap(vmap())/scatter
  85.9 3.9 %dynamic-slice_select_fusion.2 = f32[1,2,256,256]{3,2,1,0:T(8,128)S(1)} fusion(f32[1,2,256,256]{3,2,1,0:T(8,128)S(1)} %copy.105, f32[2,2,640,640]{3,2,1,0:T(8,128)} %get-tuple-element.176, s32[]{:T(128)} %bitcast.205, s32[]{:T(128)} %bitcast.206, s32[]{:T(128)} %bitcast.207, pred[]{:T(512)} %and_reduce_fusion.2), kind=kLoop, calls=%fused_computation.3.clone.1 | loop fusion | flops 131072 | bytes 1572877 | tf_op jit(solution)/shard_map/vmap(vmap())/scatter
  89.8 8.6 %dynamic-update-slice.8 = f32[2,2,640,640]{3,2,1,0:T(8,128)} dynamic-update-slice(f32[2,2,640,640]{3,2,1,0:T(8,128)} %get-tuple-element.176, f32[1,2,256,256]{3,2,1,0:T(8,128)S(1)} %dynamic-slice_select_fusion.2, s32[]{:T(128)} %bitcast.205, s32[]{:T(128)} %constant.71.clone.1..sunk, s32[]{:T(128)} %bitcast.206, s32[]{:T(128)} %bitcast.207) | dynamic-update-slice | bytes 1048580 | tf_op jit(solution)/shard_map/vmap(vmap())/scatter
  98.4 3.8 %reduce_sum.66 = bf16[2,640,640]{2,1,0:T(8,128)(2,1)S(1)} reduce(f32[2,2,640,640]{3,2,1,0:T(8,128)} %get-tuple-element.16, f32[]{:T(128)} %constant.70.clone.1), dimensions={0}, to_apply=%region_5.6 | reduce | flops 819200 | bytes 8192004 | tf_op jit(solution)/shard_map/reduce_sum | solution.py:134
  102.2 5.6 %collective-permute-start.4 = (bf16[2,64,640]{2,1,0:T(8,128)(2,1)S(1)}, bf16[2,64,640]{2,1,0:T(8,128)(2,1)S(1)}, u32[]{:S(2)}, u32[]{:S(2)}) collective-permute-start(bf16[2,64,640]{2,1,0:T(8,128)(2,1)S(1)} %get-tuple-element.69), channel_id=1, source_target_pairs={{0,2},{1,3},{4,6},{5,7},{8,10},{9,11},{12,14},{13,15},{16,18},{17,... | collective-permute-start | bytes 491528 | tf_op jit(solution)/shard_map/ppermute | solution.py:21
  107.9 1.3 collective-permute-start.5
  109.2 1.5 collective-permute-done.4
  110.7 6.3 %collective-permute-done.5 = bf16[2,64,640]{2,1,0:T(8,128)(2,1)S(1)} collective-permute-done((bf16[2,64,640]{2,1,0:T(8,128)(2,1)S(1)}, bf16[2,64,640]{2,1,0:T(8,128)(2,1)S(1)}, u32[]{:S(2)}, u32[]{:S(2)}) %collective-permute-start.5) | collective-permute-done | bytes 163872 | tf_op jit(solution)/shard_map/ppermute | solution.py:23
  117.1 1.3 collective-permute-start.6
  118.5 1.3 collective-permute-start.7
  119.8 4.3 %collective-permute-done.6 = bf16[2,768,64]{2,1,0:T(8,128)(2,1)S(1)} collective-permute-done((bf16[2,768,64]{2,1,0:T(8,128)(2,1)S(1)}, bf16[2,768,64]{2,1,0:T(8,128)(2,1)S(1)}, u32[]{:S(2)}, u32[]{:S(2)}) %collective-permute-start.6) | collective-permute-done | bytes 196640 | tf_op jit(solution)/shard_map/ppermute | solution.py:21
  124.1 4.1 %collective-permute-done.7 = bf16[2,768,64]{2,1,0:T(8,128)(2,1)S(1)} collective-permute-done((bf16[2,768,64]{2,1,0:T(8,128)(2,1)S(1)}, bf16[2,768,64]{2,1,0:T(8,128)(2,1)S(1)}, u32[]{:S(2)}, u32[]{:S(2)}) %collective-permute-start.7) | collective-permute-done | bytes 196640 | tf_op jit(solution)/shard_map/ppermute | solution.py:23
  128.3 2.0 maximum_convert_fusion
  131.0 1.8 convert_bitcast_fusion
  132.7 2.1 copy.59
  134.8 14.4 %all-to-all-start = ((bf16[1,2,512,512]{3,1,0,2:T(2,128)(2,1)}), bf16[1,2,512,512]{3,1,0,2:T(2,128)(2,1)S(1)}, u32[]{:S(2)}, u32[]{:S(2)}) async-start(bf16[1,2,512,512]{3,1,0,2:T(2,128)(2,1)} %copy.59), calls=%async_computation | async-start | bytes 2097152 | tf_op jit(solution)/shard_map/all_to_all | solution.py:152
  150.2 44.7 %all-reduce.5.cloned.1.call-done = bf16[2,2,256,256]{2,3,0,1:T(8,128)(2,1)} async-done(((bf16[2,2,256,256]{2,3,0,1:T(8,128)(2,1)}), bf16[2,2,256,256]{2,3,0,1:T(8,128)(2,1)}) %all-reduce.5.cloned.1.call-update) | async-done | bytes 524304 | tf_op jit(solution)/shard_map/psum | solution.py:140
  195.1 45.4 %all-reduce.7.cloned.1.call-done = bf16[2,2,256,256]{2,3,0,1:T(8,128)(2,1)} async-done(((bf16[2,2,256,256]{2,3,0,1:T(8,128)(2,1)}), bf16[2,2,256,256]{2,3,0,1:T(8,128)(2,1)}) %all-reduce.7.cloned.1.call-update) | async-done | bytes 524304 | tf_op jit(solution)/shard_map/psum | solution.py:140
  240.4 1.1 multiply_bitcast_fusion
  241.6 1.3 copy.66
  243.3 4.6 %bitcast_convert_fusion = bf16[64,2,4,1024]{3,0,2,1:T(8,128)(2,1)S(1)} fusion(s32[2,512]{1,0:T(2,128)S(1)} %multiply_add_fusion, bf16[64,2,2,4,512]{4,3,2,1,0:T(4,128)(2,1)S(1)} %bitcast.222), kind=kOutput, calls=%fused_computation.33 | convolution fusion | flops 1097334784 | bytes 2101248 | tf_op jit(solution)/shard_map/ascrt,stv->acrv/dot_general | solution.py:154
  248.2 1.4 copy.62
  250.6 2.9 %fusion.30 = f32[4,2,8,128]{3,0,1,2:T(4,128)S(1)} fusion(bf16[8,16,2,4,128]{4,3,2,1,0:T(4,128)(2,1)S(1)} %bitcast.221, bf16[8,16,128,128]{3,2,1,0:T(8,128)(2,1)} %param.11), kind=kOutput, calls=%fused_computation.48 | convolution fusion | flops 33554432 | bytes 4489216 | tf_op jit(solution)/shard_map/bkcru,bkuv->rcbv/dot_general | solution.py:160
  (83 shorter events, 16.3 us)
Async XLA Ops:
  7.2 14.8 %copy-start = (bf16[1,2,512,512]{3,2,1,0:T(8,128)(2,1)S(1)}, bf16[1,2,512,512]{3,2,1,0:T(8,128)(2,1)}, u32[]{:S(2)}) copy-start(bf16[1,2,512,512]{3,2,1,0:T(8,128)(2,1)} %param.6) | copy-start | bytes 3145732
  8.3 13.0 %collective-permute-start = (bf16[2,64,512]{2,1,0:T(8,128)(2,1)S(1)}, bf16[2,64,512]{2,1,0:T(8,128)(2,1)S(1)}, u32[]{:S(2)}, u32[]{:S(2)}) collective-permute-start(bf16[2,64,512]{2,1,0:T(8,128)(2,1)S(1)} %get-tuple-element.75), channel_id=1, source_target_pairs={{0,2},{1,3},{4,6},{5,7},{8,10},{9,11},{12,14},{13,15},{16,18},{17,... | collective-permute-start | bytes 393224 | tf_op jit(solution)/shard_map/ppermute | solution.py:21
  13.4 8.4 %collective-permute-start.1 = (bf16[2,64,512]{2,1,0:T(8,128)(2,1)S(1)}, bf16[2,64,512]{2,1,0:T(8,128)(2,1)S(1)}, u32[]{:S(2)}, u32[]{:S(2)}) collective-permute-start(bf16[2,64,512]{2,1,0:T(8,128)(2,1)S(1)} %get-tuple-element.76), channel_id=1, source_target_pairs={{2,0},{3,1},{6,4},{7,5},{10,8},{11,9},{14,12},{15,13},{18,16},{19,... | collective-permute-start | bytes 393224 | tf_op jit(solution)/shard_map/ppermute | solution.py:23
  21.3 11.6 %copy-start.5 = (bf16[1,256,2,256]{3,1,2,0:T(8,128)(2,1)}, bf16[1,256,2,256]{3,1,2,0:T(8,128)(2,1)S(1)}, u32[]{:S(2)}) copy-start(bf16[1,256,2,256]{3,1,2,0:T(8,128)(2,1)S(1)} %get-tuple-element.83) | copy-start | bytes 786436
  21.3 11.6 %copy-start.8 = (bf16[1,256,2,256]{3,1,2,0:T(8,128)(2,1)}, bf16[1,256,2,256]{3,1,2,0:T(8,128)(2,1)S(1)}, u32[]{:S(2)}) copy-start(bf16[1,256,2,256]{3,1,2,0:T(8,128)(2,1)S(1)} %get-tuple-element.79) | copy-start | bytes 786436
  21.3 0.7 copy-start.11
  22.0 1.0 copy-start.12
  23.0 9.9 %collective-permute-start.2 = (bf16[2,640,64]{2,1,0:T(8,128)(2,1)}, bf16[2,640,64]{2,1,0:T(8,128)(2,1)}, u32[]{:S(2)}, u32[]{:S(2)}) collective-permute-start(bf16[2,640,64]{2,1,0:T(8,128)(2,1)} %get-tuple-element.71), channel_id=1, source_target_pairs={{0,1},{2,3},{4,5},{6,7},{8,9},{10,11},{12,13},{14,15},{16,17},{18,... | collective-permute-start | bytes 491528 | tf_op jit(solution)/shard_map/ppermute | solution.py:21
  26.3 11.1 %collective-permute-start.3 = (bf16[2,640,64]{2,1,0:T(8,128)(2,1)}, bf16[2,640,64]{2,1,0:T(8,128)(2,1)}, u32[]{:S(2)}, u32[]{:S(2)}) collective-permute-start(bf16[2,640,64]{2,1,0:T(8,128)(2,1)} %get-tuple-element.72), channel_id=1, source_target_pairs={{1,0},{3,2},{5,4},{7,6},{9,8},{11,10},{13,12},{15,14},{17,16},{19,... | collective-permute-start | bytes 491528 | tf_op jit(solution)/shard_map/ppermute | solution.py:23
  39.5 7.4 %copy-start.1 = (f32[2,256,256]{1,2,0:T(8,128)S(1)}, f32[2,256,256]{1,2,0:T(8,128)}, u32[]{:S(2)}) copy-start(f32[2,256,256]{1,2,0:T(8,128)} %copy.50) | copy-start | bytes 1572868
  45.4 2.9 %copy-start.9 = (bf16[1,256,2,256]{3,1,2,0:T(8,128)(2,1)S(1)}, bf16[1,256,2,256]{3,1,2,0:T(8,128)(2,1)}, u32[]{:S(2)}) copy-start(bf16[1,256,2,256]{3,1,2,0:T(8,128)(2,1)} %copy-done.8) | copy-start | bytes 786436
  45.4 2.9 %copy-start.10 = (bf16[1,256,2,256]{3,1,2,0:T(8,128)(2,1)S(1)}, bf16[1,256,2,256]{3,1,2,0:T(8,128)(2,1)}, u32[]{:S(2)}) copy-start(bf16[1,256,2,256]{3,1,2,0:T(8,128)(2,1)} %get-tuple-element.84) | copy-start | bytes 786436
  46.8 6.5 %copy-start.3 = (f32[2,256,256]{1,2,0:T(8,128)}, f32[2,256,256]{1,2,0:T(8,128)S(1)}, u32[]{:S(2)}) copy-start(f32[2,256,256]{1,2,0:T(8,128)S(1)} %copy.49) | copy-start | bytes 1572868
  47.0 6.3 %copy-start.4 = (f32[2,256,256]{1,2,0:T(8,128)}, f32[2,256,256]{1,2,0:T(8,128)S(1)}, u32[]{:S(2)}) copy-start(f32[2,256,256]{1,2,0:T(8,128)S(1)} %copy.51) | copy-start | bytes 1572868
  48.3 6.4 %copy-start.6 = (bf16[1,1,1,2,256,256]{4,5,3,2,1,0:T(8,128)(2,1)S(1)}, bf16[1,1,1,2,256,256]{4,5,3,2,1,0:T(8,128)(2,1)}, u32[]{:S(2)}) copy-start(bf16[1,1,1,2,256,256]{4,5,3,2,1,0:T(8,128)(2,1)} %copy.54) | copy-start | bytes 786436
  55.8 3.4 %copy-start.2 = (f32[2,256,256]{1,2,0:T(8,128)S(1)}, f32[2,256,256]{1,2,0:T(8,128)}, u32[]{:S(2)}) copy-start(f32[2,256,256]{1,2,0:T(8,128)} %copy.50) | copy-start | bytes 1572868
  62.0 3.2 %copy-start.13 = (s32[4]{0:T(128)S(1)}, s32[4]{0:T(128)}, u32[]{:S(2)}) copy-start(s32[4]{0:T(128)} %constant.300) | copy-start | bytes 52
  102.2 8.4 %collective-permute-start.4 = (bf16[2,64,640]{2,1,0:T(8,128)(2,1)S(1)}, bf16[2,64,640]{2,1,0:T(8,128)(2,1)S(1)}, u32[]{:S(2)}, u32[]{:S(2)}) collective-permute-start(bf16[2,64,640]{2,1,0:T(8,128)(2,1)S(1)} %get-tuple-element.69), channel_id=1, source_target_pairs={{0,2},{1,3},{4,6},{5,7},{8,10},{9,11},{12,14},{13,15},{16,18},{17,... | collective-permute-start | bytes 491528 | tf_op jit(solution)/shard_map/ppermute | solution.py:21
  107.9 9.1 %collective-permute-start.5 = (bf16[2,64,640]{2,1,0:T(8,128)(2,1)S(1)}, bf16[2,64,640]{2,1,0:T(8,128)(2,1)S(1)}, u32[]{:S(2)}, u32[]{:S(2)}) collective-permute-start(bf16[2,64,640]{2,1,0:T(8,128)(2,1)S(1)} %get-tuple-element.70), channel_id=1, source_target_pairs={{2,0},{3,1},{6,4},{7,5},{10,8},{11,9},{14,12},{15,13},{18,16},{19,... | collective-permute-start | bytes 491528 | tf_op jit(solution)/shard_map/ppermute | solution.py:23
  117.1 6.9 %collective-permute-start.6 = (bf16[2,768,64]{2,1,0:T(8,128)(2,1)S(1)}, bf16[2,768,64]{2,1,0:T(8,128)(2,1)S(1)}, u32[]{:S(2)}, u32[]{:S(2)}) collective-permute-start(bf16[2,768,64]{2,1,0:T(8,128)(2,1)S(1)} %get-tuple-element.67), channel_id=1, source_target_pairs={{0,1},{2,3},{4,5},{6,7},{8,9},{10,11},{12,13},{14,15},{16,17},{18,... | collective-permute-start | bytes 589832 | tf_op jit(solution)/shard_map/ppermute | solution.py:21
  118.5 9.7 %collective-permute-start.7 = (bf16[2,768,64]{2,1,0:T(8,128)(2,1)S(1)}, bf16[2,768,64]{2,1,0:T(8,128)(2,1)S(1)}, u32[]{:S(2)}, u32[]{:S(2)}) collective-permute-start(bf16[2,768,64]{2,1,0:T(8,128)(2,1)S(1)} %get-tuple-element.68), channel_id=1, source_target_pairs={{1,0},{3,2},{5,4},{7,6},{9,8},{11,10},{13,12},{15,14},{17,16},{19,... | collective-permute-start | bytes 589832 | tf_op jit(solution)/shard_map/ppermute | solution.py:23
  128.3 2.0 copy-start.15
  132.7 16.5 %copy-start.7 = (bf16[2,256,256]{1,2,0:T(8,128)(2,1)S(1)}, bf16[2,256,256]{1,2,0:T(8,128)(2,1)}, u32[]{:S(2)}) copy-start(bf16[2,256,256]{1,2,0:T(8,128)(2,1)} %get-tuple-element.34) | copy-start | bytes 786436
  132.7 62.2 %copy-start.14 = (s32[8,16]{1,0:T(8,128)S(1)}, s32[8,16]{1,0:T(8,128)}, u32[]{:S(2)}) copy-start(s32[8,16]{1,0:T(8,128)} %param.10) | copy-start | bytes 1540
  134.8 108.1 %all-to-all-start = ((bf16[1,2,512,512]{3,1,0,2:T(2,128)(2,1)}), bf16[1,2,512,512]{3,1,0,2:T(2,128)(2,1)S(1)}, u32[]{:S(2)}, u32[]{:S(2)}) async-start(bf16[1,2,512,512]{3,1,0,2:T(2,128)(2,1)} %copy.59), calls=%async_computation | async-start | bytes 2097152 | tf_op jit(solution)/shard_map/all_to_all | solution.py:152
  149.2 45.7 %all-reduce.5.cloned.1.call-start = ((), (), s32[]{:S(2)}) async-start(), calls=%async_computation.1 | async-start | bytes 1048576 | tf_op jit(solution)/shard_map/psum | solution.py:140
  150.1 90.3 %all-reduce.7.cloned.1.call-start = ((), (), s32[]{:S(2)}) async-start(), calls=%async_computation.2 | async-start | bytes 1048576 | tf_op jit(solution)/shard_map/psum | solution.py:140
Sparse Core Ops, SparseCore 0:
  153.2 41.6 all-reduce.4
  197.5 42.8 all-reduce.6
